TPU v7x, 32 devices: a whole 2x2x4 slice. The times are simulated.
32 devices in a mesh: cell: 4 (over y, x), sub: 8 (over z, core).
Axes of the slice: x: 2, y: 2, z: 4, core: 2. Of those that a mesh axis runs over, the one named last changes fastest.
Arguments:
- shell_conc: float32 [4, 32, 10, 128, 128], P('cell', 'sub'), may hold values from 0.2 to 0.8
- heat_rise: float32 [4, 30, 128, 128], P('cell', None, 'sub'), may hold values from -5 to 5
- layer_current: float32 [4, 32, 128, 128], P('cell', 'sub'), may hold values from -4 to 4
- layer_counts: int32 [8], replicated, may hold values from 1 to 4, 30 in all
- contacts: int32 [4, 2], replicated, may hold values from -1 to 3, as said below
Outputs:
- conc_new: float32 [4, 32, 10, 128, 128], P('cell', 'sub')
- heat_new: float32 [4, 30, 128, 128], P('cell', None, 'sub')
Inputs may be any that keep to these rules, and one draw needn't show every extreme that they name: `layer_counts`: entry d is the number of consecutive layers held by index d of sub, in order; the entries sum to 30 and the largest is exactly 4. `contacts`: row c names the cell below and the cell above cell c in one stacking order of all 4 cells, each cell once; -1 marks the two ends of the stack.
All inputs are finite; a program needn't handle non-finite values.
Results may differ from a plain program's by a relative error of at most 0.0003.
Values sent between devices are 32-bit elements; how exact they have to be, the bound alone decides.
A program may use at most 64 MiB of HBM per device.

v0:
```python
import jax
import jax.numpy as jnp
from jax import lax
from jax.sharding import PartitionSpec as P

BASE_KELVIN = 298.15
RATE_ACTIVATION = 5000.0
DIFFUSION_ACTIVATION = 3000.0
RATE_CONSTANT = 0.5
VOLT_PER_KELVIN = 2.0 * 8.314462618 / 96485.33212
HEAT_SCALE = 10.0
ENTROPY_SLOPE = 0.001
DIFFUSION_STEP = 0.005
SURFACE_STEP = 0.005
INPLANE_CONDUCT = 0.25
THROUGH_CONDUCT = 2.0
CONTACT_CONDUCT = 0.5


def with_halo(cells, sides, width):
    for axis, dim in sides:
        count = lax.axis_size(axis)
        ends = count - 1
        head = lax.slice_in_dim(cells, 0, width, axis=dim)
        tail = lax.slice_in_dim(cells, cells.shape[dim] - width, cells.shape[dim], axis=dim)
        cells = jnp.concatenate(
            [
                lax.ppermute(tail, axis, [(i, (i + 1) % count) for i in range(ends)]),
                cells,
                lax.ppermute(head, axis, [((i + 1) % count, i) for i in range(ends)]),
            ],
            axis=dim,
        )
    return cells


def inverse_sine(value):
    magnitude = jnp.abs(value)
    rooted = jnp.sqrt(1.0 + magnitude * magnitude)
    positive = jnp.log1p(magnitude + magnitude * magnitude / (1.0 + rooted))
    return jnp.where(value < 0.0, -positive, positive)


def layer_tables(layer_counts, slot_count, layer_total):
    finish = jnp.cumsum(layer_counts)
    starts = finish - layer_counts
    devices = layer_counts.shape[0]
    device_ids = jnp.arange(devices, dtype=jnp.int32)
    slot_index = jnp.arange(devices * slot_count, dtype=jnp.int32)
    slot_owner = slot_index // slot_count
    slot_place = slot_index % slot_count
    owner_hits = slot_owner[:, None] == device_ids[None, :]
    owner_count = jnp.sum(jnp.where(owner_hits, layer_counts[None, :], 0), axis=1)
    owner_start = jnp.sum(jnp.where(owner_hits, starts[None, :], 0), axis=1)
    live_slot = slot_place < owner_count
    slot_layer = jnp.minimum(owner_start + slot_place, layer_total - 1)
    layer_index = jnp.arange(layer_total, dtype=jnp.int32)
    layer_owner = jnp.sum((finish[None, :] <= layer_index[:, None]).astype(jnp.int32), axis=1)
    layer_hits = layer_owner[:, None] == device_ids[None, :]
    layer_start = jnp.sum(jnp.where(layer_hits, starts[None, :], 0), axis=1)
    layer_slot = layer_owner * slot_count + layer_index - layer_start
    return (live_slot, slot_layer, layer_slot)


def kinetics(surface, kelvin, current):
    reciprocal = 1.0 / BASE_KELVIN - 1.0 / kelvin
    base_rate = (
        RATE_CONSTANT * jnp.exp(RATE_ACTIVATION * reciprocal) * jnp.sqrt(surface * (1.0 - surface))
    )
    ratio_rate = current / (2.0 * base_rate)
    arcsine = inverse_sine(ratio_rate)
    overvoltage = VOLT_PER_KELVIN * kelvin * arcsine
    entropic = ENTROPY_SLOPE * (0.5 - surface)
    source = HEAT_SCALE * current * (overvoltage + kelvin * entropic)
    heat_slope = (
        HEAT_SCALE
        * current
        * (
            VOLT_PER_KELVIN * arcsine
            - VOLT_PER_KELVIN
            * ratio_rate
            * RATE_ACTIVATION
            / (kelvin * jnp.sqrt(1.0 + ratio_rate * ratio_rate))
            + entropic
        )
    )
    return (source, heat_slope)


def particle(states, kelvin, current):
    shells = states.shape[1]
    speedup = jnp.exp(DIFFUSION_ACTIVATION * (1.0 / BASE_KELVIN - 1.0 / kelvin))
    volumes = [((radial + 1) ** 3 - radial**3) / (3.0 * shells**3) for radial in range(shells)]
    linkage = [
        DIFFUSION_STEP * speedup * ((radial + 1) ** 2 / shells**2 * shells)
        for radial in range(shells - 1)
    ]
    uppers = []
    values = []
    for radial in range(shells):
        diagonal = volumes[radial] + jnp.zeros_like(kelvin)
        right_side = volumes[radial] * states[:, radial]
        if radial < shells - 1:
            diagonal = diagonal + linkage[radial]
        else:
            right_side = right_side - SURFACE_STEP * current
        if radial > 0:
            diagonal = diagonal + linkage[radial - 1] - linkage[radial - 1] * uppers[radial - 1]
            right_side = right_side + linkage[radial - 1] * values[radial - 1]
        if radial < shells - 1:
            uppers.append(linkage[radial] / diagonal)
        else:
            uppers.append(jnp.zeros_like(kelvin))
        values.append(right_side / diagonal)
    result = [None] * shells
    result[shells - 1] = values[shells - 1]
    for radial in range(shells - 2, -1, -1):
        result[radial] = values[radial] + uppers[radial] * result[radial + 1]
    return jnp.stack(result, axis=1)


def column_solve(right_side, heat_slope):
    layer_total = right_side.shape[1]
    uppers = []
    values = []
    for height in range(layer_total):
        diagonal = 1.0 - heat_slope[:, height]
        source = right_side[:, height]
        if height > 0:
            diagonal = diagonal + THROUGH_CONDUCT - THROUGH_CONDUCT * uppers[height - 1]
            source = source + THROUGH_CONDUCT * values[height - 1]
        if height < layer_total - 1:
            diagonal = diagonal + THROUGH_CONDUCT
        uppers.append(THROUGH_CONDUCT / diagonal)
        values.append(source / diagonal)
    result = [None] * layer_total
    result[layer_total - 1] = values[layer_total - 1]
    for height in range(layer_total - 2, -1, -1):
        result[height] = values[height] + uppers[height] * result[height + 1]
    return jnp.stack(result, axis=1)


def per_device(shell_conc, heat_rise, layer_current, layer_counts, contacts):
    slot_count = shell_conc.shape[1]
    shells = shell_conc.shape[2]
    layer_total = heat_rise.shape[1]
    live_slot, slot_layer, layer_slot = layer_tables(layer_counts, slot_count, layer_total)
    position = lax.axis_index("sub")
    devices = lax.axis_size("sub")
    outgoing = jnp.take(heat_rise, slot_layer, axis=1)
    slot_rise = lax.all_to_all(outgoing, "sub", split_axis=1, concat_axis=2, tiled=True)
    kelvin = BASE_KELVIN + slot_rise
    surface = shell_conc[:, :, shells - 1]
    source, heat_slope = kinetics(surface, kelvin, layer_current)
    got_source, got_slope = (
        lax.all_to_all(source, "sub", split_axis=2, concat_axis=1, tiled=True),
        lax.all_to_all(heat_slope, "sub", split_axis=2, concat_axis=1, tiled=True),
    )
    layer_source = jnp.take(got_source, layer_slot, axis=1)
    layer_slope = jnp.take(got_slope, layer_slot, axis=1)
    updated = particle(shell_conc[0], kelvin[0], layer_current[0])[None]
    own_live = lax.dynamic_slice_in_dim(live_slot, position * slot_count, slot_count)
    conc_new = jnp.where(own_live[None, :, None, None, None], updated, 0.0)
    face_rows = jnp.stack([heat_rise[:, 0], heat_rise[:, layer_total - 1]], axis=1)
    every_face = lax.all_gather(face_rows, "cell", axis=0, tiled=True)
    partners = lax.dynamic_index_in_dim(contacts, lax.axis_index("cell"), 0, keepdims=False)
    lower_pair = lax.dynamic_index_in_dim(
        every_face, jnp.maximum(partners[0], 0), 0, keepdims=False
    )
    upper_pair = lax.dynamic_index_in_dim(
        every_face, jnp.maximum(partners[1], 0), 0, keepdims=False
    )
    below_face = jnp.where(partners[0] >= 0, lower_pair[1], 0.0)[None]
    above_face = jnp.where(partners[1] >= 0, upper_pair[0], 0.0)[None]
    rim_rows = with_halo(heat_rise, (("sub", 2),), 1)
    low_row = jnp.where(position == 0, heat_rise[:, :, 0:1], rim_rows[:, :, 0:1])
    high_row = jnp.where(position == devices - 1, heat_rise[:, :, -1:], rim_rows[:, :, -1:])
    column_pad = jnp.concatenate([low_row, heat_rise, high_row], axis=2)
    row_pad = jnp.pad(heat_rise, ((0, 0), (0, 0), (0, 0), (1, 1)), mode="edge")
    laplace = (
        column_pad[:, :, 2:]
        + column_pad[:, :, :-2]
        + row_pad[:, :, :, 2:]
        + row_pad[:, :, :, :-2]
        - 4.0 * heat_rise
    )
    right_side = heat_rise + INPLANE_CONDUCT * laplace + layer_source - layer_slope * heat_rise
    first_row = right_side[:, 0] + CONTACT_CONDUCT * (below_face - heat_rise[:, 0])
    last_row = right_side[:, layer_total - 1] + CONTACT_CONDUCT * (
        above_face - heat_rise[:, layer_total - 1]
    )
    right_side = jnp.concatenate(
        [first_row[:, None], right_side[:, 1 : layer_total - 1], last_row[:, None]], axis=1
    )
    heat_new = column_solve(right_side, layer_slope)
    return (conc_new, heat_new)


def solution(mesh):
    in_specs = (
        P("cell", "sub", None, None, None),
        P("cell", None, "sub", None),
        P("cell", "sub", None, None),
        P(),
        P(),
    )
    out_specs = (P("cell", "sub", None, None, None), P("cell", None, "sub", None))
    return jax.shard_map(
        per_device, mesh=mesh, in_specs=in_specs, out_specs=out_specs, check_vma=False
    )
```

profile of v0, /device:TPU:0, one launch (start us, length us, event | category | flops | bytes accessed | tf_op | source)
XLA Modules:
  0.0 71.9 jit_solution(17056215816559929877)
XLA Ops:
  0.6 1.0 %fusion.193 = (f32[1,30,1,128]{3,2,1,0:T(1,128)S(1)}, f32[1,30,1,128]{3,2,1,0:T(1,128)S(1)}) fusion(f32[1,30,16,128]{3,2,1,0:T(8,128)} %param.8), kind=kLoop, calls=%fused_computation.427 | loop fusion | bytes 61440 | tf_op jit(solution)/shard_map/slice | solution.py:176
  1.6 1.3 %collective-permute-start = (f32[1,30,1,128]{3,2,1,0:T(1,128)S(1)}, f32[1,30,1,128]{3,2,1,0:T(1,128)S(1)}, u32[]{:S(2)}, u32[]{:S(2)}) collective-permute-start(f32[1,30,1,128]{3,2,1,0:T(1,128)S(1)} %get-tuple-element.86), channel_id=1, source_target_pairs={{1,0},{2,1},{3,2},{4,3},{5,4},{6,5},{7,6},{9,8},{10,9},{11,10},{12... | collective-permute-start | bytes 46088 | tf_op jit(solution)/shard_map/ppermute | solution.py:30
  2.9 3.0 %collective-permute-start.1 = (f32[1,30,1,128]{3,2,1,0:T(1,128)S(1)}, f32[1,30,1,128]{3,2,1,0:T(1,128)S(1)}, u32[]{:S(2)}, u32[]{:S(2)}) collective-permute-start(f32[1,30,1,128]{3,2,1,0:T(1,128)S(1)} %get-tuple-element.87), channel_id=1, source_target_pairs={{0,1},{1,2},{2,3},{3,4},{4,5},{5,6},{6,7},{8,9},{9,10},{10,11},{11... | collective-permute-start | bytes 46088 | tf_op jit(solution)/shard_map/ppermute | solution.py:28
  6.0 0.8 %reduce-window.8 = s32[8,1]{0,1:T(1,128)S(1)} reduce-window(s32[8,1]{0,1:T(1,128)} %bitcast.460, s32[]{:T(128)} %constant.160.clone.1), window={size=8x1 pad=7_0x0_0}, to_apply=%region_1.2 | reduce-window | flops 56 | bytes 68 | tf_op jit(solution)/shard_map/reduce-window.3
  7.5 0.7 %select_reduce_fusion.2 = (s32[32]{0:T(128)S(1)}, s32[32]{0:T(128)S(1)}) fusion(s32[8]{0:T(128)} %param.10, s32[32]{0:T(128)S(1)} %and_select_fusion.1, s32[8]{0:T(128)S(1)} %bitcast_subtract_fusion), kind=kLoop, calls=%fused_computation.407 | loop fusion | flops 1216 | bytes 448 | tf_op jit(solution)/shard_map/reduce_sum | solution.py:53
  8.3 1.5 %gather_fusion = f32[32,16,128]{2,1,0:T(8,128)S(1)} fusion(f32[30,16,128]{2,1,0:T(8,128)} %bitcast.445, s32[1024]{0:T(1024)S(1)} %pad_clamp_fusion.1), kind=kCustom, calls=%fused_computation.2 | custom fusion | bytes 524416 | tf_op jit(solution)/shard_map/jit(_take)/gather | solution.py:150
  9.8 0.8 %bitcast_select_fusion = f32[1,32,16,128]{3,2,0,1:T(8,128)} fusion(f32[32,16,128]{2,1,0:T(8,128)S(1)} %gather_fusion, pred[32]{0:T(512)(128)(4,1)S(1)} %compare_and_fusion.1), kind=kLoop, calls=%fused_computation.119 | loop fusion | flops 65536 | bytes 524320 | tf_op jit(solution)/shard_map/jit(_take)/select_n | solution.py:150
  10.6 6.4 %all-to-all-start = ((f32[1,32,16,128]{3,2,0,1:T(8,128)}), f32[1,32,16,128]{3,2,0,1:T(8,128)S(1)}, u32[]{:S(2)}, u32[]{:S(2)}) async-start(f32[1,32,16,128]{3,2,0,1:T(8,128)} %bitcast_select_fusion), calls=%async_computation | async-start | bytes 524288 | tf_op jit(solution)/shard_map/all_to_all | solution.py:151
  16.9 0.7 fusion.195
  17.7 1.9 %fusion.194 = (f32[1,30,16,1]{3,2,1,0:T(8,128)}, f32[1,30,16,1]{3,2,1,0:T(8,128)}) fusion(f32[1,30,16,128]{3,2,1,0:T(8,128)} %param.8), kind=kLoop, calls=%fused_computation.428 | loop fusion | bytes 7680 | tf_op jit(solution)/shard_map/jit(_pad)/slice | solution.py:179
  22.9 2.0 %copy.155 = f32[1,4,10,128,128]{4,3,1,2,0:T(8,128)S(1)} copy(f32[1,4,10,128,128]{4,3,2,1,0:T(8,128)} %param.7) | data formatting | bytes 5242880 | tf_op args[0]
  25.0 8.2 %all_gather.3 = f32[4,2,16,128]{3,2,1,0:T(8,128)S(1)} all-gather(f32[1,2,16,128]{3,2,1,0:T(8,128)S(1)} %pad_maximum_fusion.4), channel_id=1, replica_groups=mesh['cell'=4,'sub'=8] {'cell'}, dimensions={0}, use_global_device_ids=true | all-gather | bytes 81920 | tf_op jit(solution)/shard_map/all_gather | solution.py:165
  33.6 0.7 copy.129
  34.4 0.7 %copy.130 = f32[1,4,8,16,128]{4,3,2,1,0:T(8,128)} copy(f32[1,4,8,16,128]{4,3,1,2,0:T(8,128)S(1)} %bitcast.453) | data formatting | bytes 524288 | tf_op jit(solution)/shard_map/mul | solution.py:95
  35.1 0.7 copy.131
  35.8 0.7 %copy.132 = f32[1,4,8,16,128]{4,3,2,1,0:T(8,128)} copy(f32[1,4,8,16,128]{4,3,1,2,0:T(8,128)S(1)} %bitcast.451) | data formatting | bytes 524288 | tf_op jit(solution)/shard_map/mul | solution.py:95
  36.5 0.7 %copy.133 = f32[1,4,8,16,128]{4,3,2,1,0:T(8,128)} copy(f32[1,4,8,16,128]{4,3,1,2,0:T(8,128)S(1)} %bitcast.450) | data formatting | bytes 524288 | tf_op jit(solution)/shard_map/mul | solution.py:95
  37.2 0.7 copy.134
  38.0 0.7 copy.135
  38.7 1.3 %fusion.33 = (f32[1,4,128,128]{3,2,1,0:T(8,128)S(1)}, f32[1,4,128,128]{3,2,1,0:T(8,128)}) fusion(f32[1,8,4,16,128]{4,3,1,2,0:T(8,128)S(1)} %copy.145, f32[1,4,128,128]{3,2,1,0:T(8,128)S(1)} %copy-done.9, f32[1,4,10,128,128]{4,3,1,2,0:T(8,128)S(1)} %copy.155), kind=kLoop, calls=%fused_computation.65 | loop fusion | flops 2162688 | bytes 1310720 | tf_op jit(solution)/shard_map/mul | solution.py:76
  39.9 0.9 %copy.150 = f32[1,4,128,128]{3,1,0,2:T(4,128)} copy(f32[1,4,128,128]{3,2,1,0:T(8,128)S(1)} %get-tuple-element.66) | data formatting | bytes 524288 | tf_op jit(solution)/shard_map/mul | solution.py:76
  40.8 5.1 %all-to-all-start.2 = ((f32[1,4,128,128]{3,1,0,2:T(4,128)}), f32[1,4,128,128]{3,1,0,2:T(4,128)}, u32[]{:S(2)}, u32[]{:S(2)}) async-start(f32[1,4,128,128]{3,1,0,2:T(4,128)} %copy.150), calls=%async_computation.2 | async-start | bytes 524288 | tf_op jit(solution)/shard_map/all_to_all | solution.py:157
  45.9 1.8 %copy.147 = f32[1,4,128,128]{3,1,0,2:T(4,128)} copy(f32[1,4,128,128]{3,2,1,0:T(8,128)} %get-tuple-element.67) | data formatting | bytes 524288 | tf_op jit(solution)/shard_map/mul | solution.py:74
  47.8 2.2 %fusion.10 = (f32[4,1,128,128]{3,2,0,1:T(8,128)S(1)}, f32[4,1,128,128]{3,2,0,1:T(8,128)S(1)}, f32[4,1,128,128]{3,2,0,1:T(8,128)S(1)}, f32[4,1,128,128]{3,2,0,1:T...) fusion(f32[4,10,128,128]{3,2,0,1:T(8,128)S(1)} %bitcast.443, ...), kind=kLoop, calls=%fused_computation.22 | loop fusion | flops 4325376 | bytes 7077888 | tf_op jit(solution)/shard_map/div | solution.py:114
  50.1 0.7 multiply_add_fusion.1
  51.5 4.2 %all-to-all-done.2 = f32[1,4,128,128]{3,1,0,2:T(4,128)} async-done(((f32[1,4,128,128]{3,1,0,2:T(4,128)}), f32[1,4,128,128]{3,1,0,2:T(4,128)}, u32[]{:S(2)}, u32[]{:S(2)}) %all-to-all-start.2) | async-done | bytes 262176 | tf_op jit(solution)/shard_map/all_to_all | solution.py:157
  55.7 3.4 %all-to-all-start.1 = ((f32[1,4,128,128]{3,1,0,2:T(4,128)}), f32[1,4,128,128]{3,1,0,2:T(4,128)S(1)}, u32[]{:S(2)}, u32[]{:S(2)}) async-start(f32[1,4,128,128]{3,1,0,2:T(4,128)} %copy.147), calls=%async_computation.1 | async-start | bytes 524288 | tf_op jit(solution)/shard_map/all_to_all | solution.py:156
  59.1 1.0 %bitcast_dynamic-update-slice_fusion.9 = f32[1,4,10,128,128]{4,3,2,1,0:T(8,128)S(1)} fusion(f32[1,4,10,128,128]{4,3,2,1,0:T(8,128)S(1)} %bitcast_dynamic-update-slice_fusion, f32[4,1,128,128]{3,2,0,1:T(8,128)} %copy-done.8), kind=kLoop, calls=%fused_computation.66 | loop fusion | bytes 524288 | tf_op jit(solution)/shard_map/stack | solution.py:119
  60.1 1.8 %broadcast_select_fusion = f32[1,4,10,128,128]{4,3,2,1,0:T(8,128)} fusion(f32[1,4,10,128,128]{4,3,2,1,0:T(8,128)S(1)} %bitcast_dynamic-update-slice_fusion.9, pred[4]{0:T(512)(128)(4,1)S(1)} %dynamic_slice.14), kind=kLoop, calls=%fused_computation.3 | loop fusion | flops 655360 | bytes 5242884 | tf_op jit(solution)/shard_map/jit(_where)/select_n | solution.py:163
  62.0 1.0 %copy.151 = f32[1,4,128,128]{3,2,1,0:T(8,128)S(1)} copy(f32[1,4,128,128]{3,1,0,2:T(4,128)} %all-to-all-done.2) | data formatting | bytes 524288 | tf_op jit(solution)/shard_map/all_to_all | solution.py:157
  63.0 5.8 %all-to-all-done.1 = f32[1,4,128,128]{3,1,0,2:T(4,128)S(1)} async-done(((f32[1,4,128,128]{3,1,0,2:T(4,128)}), f32[1,4,128,128]{3,1,0,2:T(4,128)S(1)}, u32[]{:S(2)}, u32[]{:S(2)}) %all-to-all-start.1) | async-done | bytes 262176 | tf_op jit(solution)/shard_map/all_to_all | solution.py:156
  71.2 0.7 copy-done.14
  (96 shorter events, 4.8 us)
Async XLA Ops:
  0.6 19.1 %copy-start = (s32[4,2]{0,1:T(2,128)S(1)}, s32[4,2]{0,1:T(2,128)}, u32[]{:S(2)}) copy-start(s32[4,2]{0,1:T(2,128)} %param.11) | copy-start | bytes 100
  1.6 31.6 %collective-permute-start = (f32[1,30,1,128]{3,2,1,0:T(1,128)S(1)}, f32[1,30,1,128]{3,2,1,0:T(1,128)S(1)}, u32[]{:S(2)}, u32[]{:S(2)}) collective-permute-start(f32[1,30,1,128]{3,2,1,0:T(1,128)S(1)} %get-tuple-element.86), channel_id=1, source_target_pairs={{1,0},{2,1},{3,2},{4,3},{5,4},{6,5},{7,6},{9,8},{10,9},{11,10},{12... | collective-permute-start | bytes 46088 | tf_op jit(solution)/shard_map/ppermute | solution.py:30
  2.9 30.3 %collective-permute-start.1 = (f32[1,30,1,128]{3,2,1,0:T(1,128)S(1)}, f32[1,30,1,128]{3,2,1,0:T(1,128)S(1)}, u32[]{:S(2)}, u32[]{:S(2)}) collective-permute-start(f32[1,30,1,128]{3,2,1,0:T(1,128)S(1)} %get-tuple-element.87), channel_id=1, source_target_pairs={{0,1},{1,2},{2,3},{3,4},{4,5},{5,6},{6,7},{8,9},{9,10},{10,11},{11... | collective-permute-start | bytes 46088 | tf_op jit(solution)/shard_map/ppermute | solution.py:28
  10.6 22.7 %all-to-all-start = ((f32[1,32,16,128]{3,2,0,1:T(8,128)}), f32[1,32,16,128]{3,2,0,1:T(8,128)S(1)}, u32[]{:S(2)}, u32[]{:S(2)}) async-start(f32[1,32,16,128]{3,2,0,1:T(8,128)} %bitcast_select_fusion), calls=%async_computation | async-start | bytes 524288 | tf_op jit(solution)/shard_map/all_to_all | solution.py:151
  22.9 10.3 %copy-start.1 = (f32[1,30,16,128]{3,2,1,0:T(8,128)S(1)}, f32[1,30,16,128]{3,2,1,0:T(8,128)}, u32[]{:S(2)}) copy-start(f32[1,30,16,128]{3,2,1,0:T(8,128)} %param.8) | copy-start | bytes 737284
  33.6 5.1 %copy-start.9 = (f32[1,4,128,128]{3,2,1,0:T(8,128)S(1)}, f32[1,4,128,128]{3,2,1,0:T(8,128)}, u32[]{:S(2)}) copy-start(f32[1,4,128,128]{3,2,1,0:T(8,128)} %param.9) | copy-start | bytes 786436
  40.8 14.9 %all-to-all-start.2 = ((f32[1,4,128,128]{3,1,0,2:T(4,128)}), f32[1,4,128,128]{3,1,0,2:T(4,128)}, u32[]{:S(2)}, u32[]{:S(2)}) async-start(f32[1,4,128,128]{3,1,0,2:T(4,128)} %copy.150), calls=%async_computation.2 | async-start | bytes 524288 | tf_op jit(solution)/shard_map/all_to_all | solution.py:157
  47.7 2.3 %copy-start.2 = (f32[1,4,8,16,128]{4,3,2,1,0:T(8,128)S(1)}, f32[1,4,8,16,128]{4,3,2,1,0:T(8,128)}, u32[]{:S(2)}) copy-start(f32[1,4,8,16,128]{4,3,2,1,0:T(8,128)} %copy.129) | copy-start | bytes 786436
  47.7 2.3 %copy-start.3 = (f32[1,4,8,16,128]{4,3,2,1,0:T(8,128)S(1)}, f32[1,4,8,16,128]{4,3,2,1,0:T(8,128)}, u32[]{:S(2)}) copy-start(f32[1,4,8,16,128]{4,3,2,1,0:T(8,128)} %copy.130) | copy-start | bytes 786436
  47.7 2.3 %copy-start.4 = (f32[1,4,8,16,128]{4,3,2,1,0:T(8,128)S(1)}, f32[1,4,8,16,128]{4,3,2,1,0:T(8,128)}, u32[]{:S(2)}) copy-start(f32[1,4,8,16,128]{4,3,2,1,0:T(8,128)} %copy.131) | copy-start | bytes 786436
  47.7 2.3 %copy-start.5 = (f32[1,4,8,16,128]{4,3,2,1,0:T(8,128)S(1)}, f32[1,4,8,16,128]{4,3,2,1,0:T(8,128)}, u32[]{:S(2)}) copy-start(f32[1,4,8,16,128]{4,3,2,1,0:T(8,128)} %copy.132) | copy-start | bytes 786436
  47.7 2.3 %copy-start.6 = (f32[1,4,8,16,128]{4,3,2,1,0:T(8,128)S(1)}, f32[1,4,8,16,128]{4,3,2,1,0:T(8,128)}, u32[]{:S(2)}) copy-start(f32[1,4,8,16,128]{4,3,2,1,0:T(8,128)} %copy.133) | copy-start | bytes 786436
  47.8 2.3 %copy-start.7 = (f32[1,4,8,16,128]{4,3,2,1,0:T(8,128)S(1)}, f32[1,4,8,16,128]{4,3,2,1,0:T(8,128)}, u32[]{:S(2)}) copy-start(f32[1,4,8,16,128]{4,3,2,1,0:T(8,128)} %copy.134) | copy-start | bytes 786436
  47.8 2.3 %copy-start.10 = (f32[1,4,128,128]{3,2,1,0:T(8,128)S(1)}, f32[1,4,128,128]{3,2,1,0:T(8,128)}, u32[]{:S(2)}) copy-start(f32[1,4,128,128]{3,2,1,0:T(8,128)} %param.9) | copy-start | bytes 786436
  47.8 2.3 %copy-start.11 = (f32[1,4,8,16,128]{4,3,2,1,0:T(8,128)S(1)}, f32[1,4,8,16,128]{4,3,2,1,0:T(8,128)}, u32[]{:S(2)}) copy-start(f32[1,4,8,16,128]{4,3,2,1,0:T(8,128)} %copy.135) | copy-start | bytes 786436
  50.7 0.7 copy-start.8
  55.7 13.1 %all-to-all-start.1 = ((f32[1,4,128,128]{3,1,0,2:T(4,128)}), f32[1,4,128,128]{3,1,0,2:T(4,128)S(1)}, u32[]{:S(2)}, u32[]{:S(2)}) async-start(f32[1,4,128,128]{3,1,0,2:T(4,128)} %copy.147), calls=%async_computation.1 | async-start | bytes 524288 | tf_op jit(solution)/shard_map/all_to_all | solution.py:156
  62.0 8.1 %copy-start.12 = (f32[1,30,16,1]{3,2,1,0:T(8,128)S(1)}, f32[1,30,16,1]{3,2,1,0:T(8,128)}, u32[]{:S(2)}) copy-start(f32[1,30,16,1]{3,2,1,0:T(8,128)} %get-tuple-element.88) | copy-start | bytes 5764
  62.0 8.1 %copy-start.13 = (f32[1,30,16,1]{3,2,1,0:T(8,128)S(1)}, f32[1,30,16,1]{3,2,1,0:T(8,128)}, u32[]{:S(2)}) copy-start(f32[1,30,16,1]{3,2,1,0:T(8,128)} %get-tuple-element.89) | copy-start | bytes 5764
  71.2 0.7 copy-start.14
where the time goes:
time: 72.6 us; the launch traced here: 71.9 us
  local copies, waits for them, and re-layouts  20 us (28%)
  starting transfers between devices  19.2 us (26%)
  other arithmetic  10.6 us (15%)
  waiting for transfers between devices  10 us (14%)
  blocking collectives  8.23 us (11%)
  between operations  3.8 us (5%)
    all_gather x1, blocking collectives, per_device(): every_face = lax.all_gather(face_rows, 'cell', axis=0, tiled=True)  8.23 us
    all_to_all x1, starting transfers between devices, per_device(): lax.all_to_all(outgoing, 'sub', split_axis=1, concat_axis=2, tiled=True)  6.35 us
    all_to_all x1, waiting for transfers between devices, per_device(): lax.all_to_all(source, 'sub', split_axis=2, concat_axis=1, tiled=True)  5.76 us
    all_to_all x1, starting transfers between devices, per_device(): lax.all_to_all(heat_slope, 'sub', split_axis=2, concat_axis=1, tiled=True)  5.1 us
    mul x9, local copies, waits for them, and re-layouts, particle(): DIFFUSION_STEP * speedup * ((radial + 1) ** 2 / shells ** 2 * shells)  5.07 us
    all_to_all x1, waiting for transfers between devices, per_device(): lax.all_to_all(heat_slope, 'sub', split_axis=2, concat_axis=1, tiled=True)  4.23 us
    all_to_all x1, starting transfers between devices, per_device(): lax.all_to_all(source, 'sub', split_axis=2, concat_axis=1, tiled=True)  3.41 us
    unnamed x50, local copies, waits for them, and re-layouts  3.22 us
  transfers between devices with their start and end apart: 5, of which 2 were waited for; matrix products, arithmetic and copies ran while one was open for 26% of the time, Pallas kernels for 0%

commit v1 on v0

--- a/solution.py
+++ b/solution.py
@@ -154,7 +154,12 @@
     source, heat_slope = kinetics(surface, kelvin, layer_current)
     got_source, got_slope = (
         lax.all_to_all(source, "sub", split_axis=2, concat_axis=1, tiled=True),
-        lax.all_to_all(heat_slope, "sub", split_axis=2, concat_axis=1, tiled=True),
+        jnp.concatenate(
+            lax.all_to_all(
+                jnp.stack(jnp.split(heat_slope, lax.axis_size("sub"), axis=2)), "sub", 0, 0
+            ),
+            axis=1,
+        ),
     )
     layer_source = jnp.take(got_source, layer_slot, axis=1)
     layer_slope = jnp.take(got_slope, layer_slot, axis=1)

time: 72.6 us -> 75.8 us (1.044)
  waiting for transfers between devices: 10 us -> 5.2 us
  local copies, waits for them, and re-layouts: 20 us -> 24.7 us
  starting transfers between devices: 19.2 us -> 20.9 us
  other arithmetic: 10.6 us -> 11.6 us
    unnamed x50 -> x57, local copies, waits for them, and re-layouts: 3.22 us -> 8.99 us
    all_to_all x1, waiting for transfers between devices: 5.76 us -> 0.01 us  [per_device(): lax.all_to_all(source, 'sub', split_axis=2, concat_axis=1, tiled=True)]
    all_to_all x1, starting transfers between devices: 3.41 us -> 5.1 us  [per_device(): lax.all_to_all(source, 'sub', split_axis=2, concat_axis=1, tiled=True)]
    all_to_all x2 -> x0, local copies, waits for them, and re-layouts: 1.04 us -> none  [per_device(): lax.all_to_all(heat_slope, 'sub', split_axis=2, concat_axis=1, tiled=True)]
    mul x1, local copies, waits for them, and re-layouts: 1.82 us -> 0.86 us  [kinetics(): source = HEAT_SCALE * current * (overvoltage + kelvin * entropic)]
    all_to_all x1, waiting for transfers between devices: 4.23 us -> 5.18 us  [per_device(): lax.all_to_all(jnp.stack(jnp.split(heat_slope, lax.axis_size('sub'), axis...]
    all_to_all x2, local copies, waits for them, and re-layouts: 0.04 us -> 0.99 us  [per_device(): lax.all_to_all(source, 'sub', split_axis=2, concat_axis=1, tiled=True)]
    select_n x1, other arithmetic: 0.32 us -> 1.25 us  [per_device(): layer_slope = jnp.take(got_slope, layer_slot, axis=1)]
  transfers between devices with their start and end apart: 5 -> 5, of which waited for: 2 -> 1; matrix products, arithmetic and copies ran while one was open for 26% -> 32% of each run, Pallas kernels for 0% -> 0%
where the time goes in v1:
time: 75.8 us; the launch traced here: 74.4 us
  local copies, waits for them, and re-layouts  24.7 us (33%)
  starting transfers between devices  20.9 us (28%)
  other arithmetic  11.6 us (15%)
  blocking collectives  8.23 us (11%)
  waiting for transfers between devices  5.2 us (7%)
  between operations  3.81 us (5%)
    unnamed x57, local copies, waits for them, and re-layouts  8.99 us
    all_gather x1, blocking collectives, per_device(): every_face = lax.all_gather(face_rows, 'cell', axis=0, tiled=True)  8.23 us
    all_to_all x1, starting transfers between devices, per_device(): lax.all_to_all(outgoing, 'sub', split_axis=1, concat_axis=2, tiled=True)  6.35 us
    all_to_all x1, waiting for transfers between devices, per_device(): lax.all_to_all(jnp.stack(jnp.split(heat_slope, lax.axis_size('sub'), axis...  5.18 us
    all_to_all x1, starting transfers between devices, per_device(): lax.all_to_all(jnp.stack(jnp.split(heat_slope, lax.axis_size('sub'), axis...  5.11 us
    all_to_all x1, starting transfers between devices, per_device(): lax.all_to_all(source, 'sub', split_axis=2, concat_axis=1, tiled=True)  5.1 us
    mul x9, local copies, waits for them, and re-layouts, particle(): DIFFUSION_STEP * speedup * ((radial + 1) ** 2 / shells ** 2 * shells)  5.08 us
    ppermute x1, starting transfers between devices, with_halo(): lax.ppermute(tail, axis, [(i, (i + 1) % count) for i in range(ends)])  3.03 us
  transfers between devices with their start and end apart: 5, of which 1 were waited for; matrix products, arithmetic and copies ran while one was open for 32% of the time, Pallas kernels for 0%

profile of v1, /device:TPU:0, one launch (start us, length us, event | category | flops | bytes accessed | tf_op | source)
XLA Modules:
  0.0 74.4 jit_solution(6996664453415383814)
XLA Ops:
  0.6 1.0 %fusion.193 = (f32[1,30,1,128]{3,2,1,0:T(1,128)S(1)}, f32[1,30,1,128]{3,2,1,0:T(1,128)S(1)}) fusion(f32[1,30,16,128]{3,2,1,0:T(8,128)} %param.8), kind=kLoop, calls=%fused_computation.443 | loop fusion | bytes 61440 | tf_op jit(solution)/shard_map/slice | solution.py:181
  1.6 1.3 %collective-permute-start = (f32[1,30,1,128]{3,2,1,0:T(1,128)S(1)}, f32[1,30,1,128]{3,2,1,0:T(1,128)S(1)}, u32[]{:S(2)}, u32[]{:S(2)}) collective-permute-start(f32[1,30,1,128]{3,2,1,0:T(1,128)S(1)} %get-tuple-element.86), channel_id=1, source_target_pairs={{1,0},{2,1},{3,2},{4,3},{5,4},{6,5},{7,6},{9,8},{10,9},{11,10},{12... | collective-permute-start | bytes 46088 | tf_op jit(solution)/shard_map/ppermute | solution.py:30
  2.9 3.0 %collective-permute-start.1 = (f32[1,30,1,128]{3,2,1,0:T(1,128)S(1)}, f32[1,30,1,128]{3,2,1,0:T(1,128)S(1)}, u32[]{:S(2)}, u32[]{:S(2)}) collective-permute-start(f32[1,30,1,128]{3,2,1,0:T(1,128)S(1)} %get-tuple-element.87), channel_id=1, source_target_pairs={{0,1},{1,2},{2,3},{3,4},{4,5},{5,6},{6,7},{8,9},{9,10},{10,11},{11... | collective-permute-start | bytes 46088 | tf_op jit(solution)/shard_map/ppermute | solution.py:28
  6.0 0.8 %reduce-window.8 = s32[8,1]{0,1:T(1,128)S(1)} reduce-window(s32[8,1]{0,1:T(1,128)} %bitcast.488, s32[]{:T(128)} %constant.160.clone.1), window={size=8x1 pad=7_0x0_0}, to_apply=%region_1.2 | reduce-window | flops 56 | bytes 68 | tf_op jit(solution)/shard_map/reduce-window.3
  7.5 0.7 select_reduce_fusion.2
  8.3 1.5 %gather_fusion = f32[32,16,128]{2,1,0:T(8,128)S(1)} fusion(f32[30,16,128]{2,1,0:T(8,128)} %bitcast.474, s32[1024]{0:T(1024)S(1)} %pad_clamp_fusion.1), kind=kCustom, calls=%fused_computation.2 | custom fusion | bytes 524416 | tf_op jit(solution)/shard_map/jit(_take)/gather | solution.py:150
  9.8 0.8 %bitcast_select_fusion = f32[1,32,16,128]{3,2,0,1:T(8,128)} fusion(f32[32,16,128]{2,1,0:T(8,128)S(1)} %gather_fusion, pred[32]{0:T(512)(128)(4,1)S(1)} %compare_and_fusion.1), kind=kLoop, calls=%fused_computation.119 | loop fusion | flops 65536 | bytes 524320 | tf_op jit(solution)/shard_map/jit(_take)/select_n | solution.py:150
  10.6 6.4 %all-to-all-start = ((f32[1,32,16,128]{3,2,0,1:T(8,128)}), f32[1,32,16,128]{3,2,0,1:T(8,128)S(1)}, u32[]{:S(2)}, u32[]{:S(2)}) async-start(f32[1,32,16,128]{3,2,0,1:T(8,128)} %bitcast_select_fusion), calls=%async_computation | async-start | bytes 524288 | tf_op jit(solution)/shard_map/all_to_all | solution.py:151
  17.7 1.9 %fusion.194 = (f32[1,30,16,1]{3,2,1,0:T(8,128)}, f32[1,30,16,1]{3,2,1,0:T(8,128)}) fusion(f32[1,30,16,128]{3,2,1,0:T(8,128)} %param.8), kind=kLoop, calls=%fused_computation.444 | loop fusion | bytes 7680 | tf_op jit(solution)/shard_map/jit(_pad)/slice | solution.py:184
  22.9 2.1 %copy.226 = f32[1,4,10,128,128]{4,3,1,2,0:T(8,128)S(1)} copy(f32[1,4,10,128,128]{4,3,2,1,0:T(8,128)} %param.7) | data formatting | bytes 5242880 | tf_op args[0]
  25.1 8.2 %all_gather.3 = f32[4,2,16,128]{3,2,1,0:T(8,128)S(1)} all-gather(f32[1,2,16,128]{3,2,1,0:T(8,128)S(1)} %pad_maximum_fusion.4), channel_id=1, replica_groups=mesh['cell'=4,'sub'=8] {'cell'}, dimensions={0}, use_global_device_ids=true | all-gather | bytes 81920 | tf_op jit(solution)/shard_map/all_gather | solution.py:170
  36.6 0.7 copy.207
  37.4 0.7 copy.208
  38.1 0.7 copy.209
  38.8 1.3 %fusion.33 = (f32[1,4,128,128]{3,2,1,0:T(8,128)}, f32[1,4,128,128]{3,2,1,0:T(8,128)S(1)}) fusion(f32[1,8,4,16,128]{4,3,1,2,0:T(8,128)S(1)} %copy.219, f32[1,4,128,128]{3,2,1,0:T(8,128)S(1)} %copy-done.9, f32[1,4,10,128,128]{4,3,1,2,0:T(8,128)S(1)} %copy.226), kind=kLoop, calls=%fused_computation.65 | loop fusion | flops 2162688 | bytes 1310720 | tf_op jit(solution)/shard_map/mul | solution.py:76
  40.1 0.9 %copy.221 = f32[1,4,128,128]{3,1,0,2:T(4,128)} copy(f32[1,4,128,128]{3,2,1,0:T(8,128)S(1)} %get-tuple-element.67) | data formatting | bytes 524288 | tf_op jit(solution)/shard_map/mul | solution.py:74
  40.9 5.1 %all-to-all-start.1 = ((f32[1,4,128,128]{3,1,0,2:T(4,128)}), f32[1,4,128,128]{3,1,0,2:T(4,128)}, u32[]{:S(2)}, u32[]{:S(2)}) async-start(f32[1,4,128,128]{3,1,0,2:T(4,128)} %copy.221), calls=%async_computation.1 | async-start | bytes 524288 | tf_op jit(solution)/shard_map/all_to_all | solution.py:156
  46.0 0.8 %constant_dynamic-update-slice_fusion.7 = f32[8,1,4,16,128]{4,3,2,1,0:T(8,128)S(1)} fusion(f32[1,4,128,128]{3,2,1,0:T(8,128)} %get-tuple-element.66), kind=kLoop, calls=%fused_computation.163 | loop fusion | bytes 65536
  46.8 0.8 %constant_dynamic-update-slice_fusion.6 = f32[8,1,4,16,128]{4,3,2,1,0:T(8,128)S(1)} fusion(f32[8,1,4,16,128]{4,3,2,1,0:T(8,128)S(1)} %constant_dynamic-update-slice_fusion.7, f32[1,4,128,128]{3,2,1,0:T(8,128)} %get-tuple-element.66), kind=kLoop, calls=%fused_computation.162 | loop fusion | bytes 65536
  47.5 0.8 %constant_dynamic-update-slice_fusion.5 = f32[8,1,4,16,128]{4,3,2,1,0:T(8,128)S(1)} fusion(f32[8,1,4,16,128]{4,3,2,1,0:T(8,128)S(1)} %constant_dynamic-update-slice_fusion.6, f32[1,4,128,128]{3,2,1,0:T(8,128)} %get-tuple-element.66), kind=kLoop, calls=%fused_computation.161 | loop fusion | bytes 65536
  48.3 0.8 %constant_dynamic-update-slice_fusion.4 = f32[8,1,4,16,128]{4,3,2,1,0:T(8,128)S(1)} fusion(f32[8,1,4,16,128]{4,3,2,1,0:T(8,128)S(1)} %constant_dynamic-update-slice_fusion.5, f32[1,4,128,128]{3,2,1,0:T(8,128)} %get-tuple-element.66), kind=kLoop, calls=%fused_computation.160 | loop fusion | bytes 65536
  49.1 0.8 %constant_dynamic-update-slice_fusion.3 = f32[8,1,4,16,128]{4,3,2,1,0:T(8,128)S(1)} fusion(f32[8,1,4,16,128]{4,3,2,1,0:T(8,128)S(1)} %constant_dynamic-update-slice_fusion.4, f32[1,4,128,128]{3,2,1,0:T(8,128)} %get-tuple-element.66), kind=kLoop, calls=%fused_computation.159 | loop fusion | bytes 65536
  49.8 0.8 %constant_dynamic-update-slice_fusion.2 = f32[8,1,4,16,128]{4,3,2,1,0:T(8,128)S(1)} fusion(f32[8,1,4,16,128]{4,3,2,1,0:T(8,128)S(1)} %constant_dynamic-update-slice_fusion.3, f32[1,4,128,128]{3,2,1,0:T(8,128)} %get-tuple-element.66), kind=kLoop, calls=%fused_computation.158 | loop fusion | bytes 65536
  50.6 0.8 %constant_dynamic-update-slice_fusion.1 = f32[8,1,4,16,128]{4,3,2,1,0:T(8,128)S(1)} fusion(f32[8,1,4,16,128]{4,3,2,1,0:T(8,128)S(1)} %constant_dynamic-update-slice_fusion.2, f32[1,4,128,128]{3,2,1,0:T(8,128)} %get-tuple-element.66), kind=kLoop, calls=%fused_computation.157 | loop fusion | bytes 65536
  51.4 2.2 %fusion.10 = (f32[4,1,128,128]{3,2,0,1:T(8,128)S(1)}, f32[4,1,128,128]{3,2,0,1:T(8,128)S(1)}, f32[4,1,128,128]{3,2,0,1:T(8,128)S(1)}, f32[4,1,128,128]{3,2,0,1:T...) fusion(f32[4,10,128,128]{3,2,0,1:T(8,128)S(1)} %bitcast.472, ...), kind=kLoop, calls=%fused_computation.22 | loop fusion | flops 4325376 | bytes 7077888 | tf_op jit(solution)/shard_map/div | solution.py:114
  54.7 0.8 %constant_dynamic-update-slice_fusion = f32[8,1,4,16,128]{4,3,2,1,0:T(8,128)S(1)} fusion(f32[8,1,4,16,128]{4,3,2,1,0:T(8,128)S(1)} %constant_dynamic-update-slice_fusion.1, f32[1,4,128,128]{3,2,1,0:T(8,128)} %get-tuple-element.66), kind=kLoop, calls=%fused_computation.156 | loop fusion | bytes 65536 | tf_op jit(solution)/shard_map/stack | solution.py:159
  56.2 5.1 %all-to-all-start.2 = ((f32[8,1,4,16,128]{4,3,2,1,0:T(8,128)}), f32[8,1,4,16,128]{4,3,2,1,0:T(8,128)S(1)}, u32[]{:S(2)}, u32[]{:S(2)}) async-start(f32[8,1,4,16,128]{4,3,2,1,0:T(8,128)} %copy-done.13), calls=%async_computation.2 | async-start | bytes 524288 | tf_op jit(solution)/shard_map/all_to_all | solution.py:158
  61.3 1.0 %bitcast_dynamic-update-slice_fusion.9 = f32[1,4,10,128,128]{4,3,2,1,0:T(8,128)S(1)} fusion(f32[1,4,10,128,128]{4,3,2,1,0:T(8,128)S(1)} %bitcast_dynamic-update-slice_fusion, f32[4,1,128,128]{3,2,0,1:T(8,128)} %copy-done.8), kind=kLoop, calls=%fused_computation.66 | loop fusion | bytes 524288 | tf_op jit(solution)/shard_map/stack | solution.py:119
  62.3 2.0 %broadcast_select_fusion = f32[1,4,10,128,128]{4,3,2,1,0:T(8,128)} fusion(f32[1,4,10,128,128]{4,3,2,1,0:T(8,128)S(1)} %bitcast_dynamic-update-slice_fusion.9, pred[4]{0:T(512)(128)(4,1)S(1)} %dynamic_slice.14), kind=kLoop, calls=%fused_computation.3 | loop fusion | flops 655360 | bytes 5242884 | tf_op jit(solution)/shard_map/jit(_where)/select_n | solution.py:168
  64.3 1.0 %copy.222 = f32[1,4,128,128]{3,2,1,0:T(8,128)S(1)} copy(f32[1,4,128,128]{3,1,0,2:T(4,128)} %all-to-all-done.1) | data formatting | bytes 524288 | tf_op jit(solution)/shard_map/all_to_all | solution.py:156
  65.9 5.2 %all-to-all-done.2 = f32[8,1,4,16,128]{4,3,2,1,0:T(8,128)S(1)} async-done(((f32[8,1,4,16,128]{4,3,2,1,0:T(8,128)}), f32[8,1,4,16,128]{4,3,2,1,0:T(8,128)S(1)}, u32[]{:S(2)}, u32[]{:S(2)}) %all-to-all-start.2) | async-done | bytes 262176 | tf_op jit(solution)/shard_map/all_to_all | solution.py:158
  71.7 1.2 %bitcast_select_fusion.1 = (f32[1,30,16,128]{3,2,1,0:T(8,128)S(1)}, f32[1,30,16,128]{3,2,1,0:T(8,128)S(1)}) fusion(f32[30,16,128]{2,1,0:T(8,128)S(1)} %gather_fusion.2, pred[30]{0:T(512)(128)(4,1)S(1)} %get-tuple-element.48, f32[1,30,16,128]{3,2,1,0:T(8,128)S(1)} %copy-done.1, f32[30,16,128]{2,1,0:T(8,128)S(1)} %gather_fusion.1, ...), kind=kLoop, calls=%fused_computation.144 | loop fusion | flops 983040 | bytes 1263390 | tf_op jit(solution)/shard_map/jit(_take)/select_n | solution.py:165
  (101 shorter events, 9.7 us)
Async XLA Ops:
  0.6 19.1 %copy-start = (s32[4,2]{0,1:T(2,128)S(1)}, s32[4,2]{0,1:T(2,128)}, u32[]{:S(2)}) copy-start(s32[4,2]{0,1:T(2,128)} %param.11) | copy-start | bytes 100
  1.6 31.7 %collective-permute-start = (f32[1,30,1,128]{3,2,1,0:T(1,128)S(1)}, f32[1,30,1,128]{3,2,1,0:T(1,128)S(1)}, u32[]{:S(2)}, u32[]{:S(2)}) collective-permute-start(f32[1,30,1,128]{3,2,1,0:T(1,128)S(1)} %get-tuple-element.86), channel_id=1, source_target_pairs={{1,0},{2,1},{3,2},{4,3},{5,4},{6,5},{7,6},{9,8},{10,9},{11,10},{12... | collective-permute-start | bytes 46088 | tf_op jit(solution)/shard_map/ppermute | solution.py:30
  2.9 30.4 %collective-permute-start.1 = (f32[1,30,1,128]{3,2,1,0:T(1,128)S(1)}, f32[1,30,1,128]{3,2,1,0:T(1,128)S(1)}, u32[]{:S(2)}, u32[]{:S(2)}) collective-permute-start(f32[1,30,1,128]{3,2,1,0:T(1,128)S(1)} %get-tuple-element.87), channel_id=1, source_target_pairs={{0,1},{1,2},{2,3},{3,4},{4,5},{5,6},{6,7},{8,9},{9,10},{10,11},{11... | collective-permute-start | bytes 46088 | tf_op jit(solution)/shard_map/ppermute | solution.py:28
  10.6 22.8 %all-to-all-start = ((f32[1,32,16,128]{3,2,0,1:T(8,128)}), f32[1,32,16,128]{3,2,0,1:T(8,128)S(1)}, u32[]{:S(2)}, u32[]{:S(2)}) async-start(f32[1,32,16,128]{3,2,0,1:T(8,128)} %bitcast_select_fusion), calls=%async_computation | async-start | bytes 524288 | tf_op jit(solution)/shard_map/all_to_all | solution.py:151
  22.9 10.4 %copy-start.1 = (f32[1,30,16,128]{3,2,1,0:T(8,128)S(1)}, f32[1,30,16,128]{3,2,1,0:T(8,128)}, u32[]{:S(2)}) copy-start(f32[1,30,16,128]{3,2,1,0:T(8,128)} %param.8) | copy-start | bytes 737284
  33.7 5.1 %copy-start.9 = (f32[1,4,128,128]{3,2,1,0:T(8,128)S(1)}, f32[1,4,128,128]{3,2,1,0:T(8,128)}, u32[]{:S(2)}) copy-start(f32[1,4,128,128]{3,2,1,0:T(8,128)} %param.9) | copy-start | bytes 786436
  40.9 15.3 %all-to-all-start.1 = ((f32[1,4,128,128]{3,1,0,2:T(4,128)}), f32[1,4,128,128]{3,1,0,2:T(4,128)}, u32[]{:S(2)}, u32[]{:S(2)}) async-start(f32[1,4,128,128]{3,1,0,2:T(4,128)} %copy.221), calls=%async_computation.1 | async-start | bytes 524288 | tf_op jit(solution)/shard_map/all_to_all | solution.py:156
  51.4 2.3 %copy-start.2 = (f32[1,4,8,16,128]{4,3,2,1,0:T(8,128)S(1)}, f32[1,4,8,16,128]{4,3,2,1,0:T(8,128)}, u32[]{:S(2)}) copy-start(f32[1,4,8,16,128]{4,3,2,1,0:T(8,128)} %copy.203) | copy-start | bytes 786436
  51.4 2.3 %copy-start.3 = (f32[1,4,8,16,128]{4,3,2,1,0:T(8,128)S(1)}, f32[1,4,8,16,128]{4,3,2,1,0:T(8,128)}, u32[]{:S(2)}) copy-start(f32[1,4,8,16,128]{4,3,2,1,0:T(8,128)} %copy.204) | copy-start | bytes 786436
  51.4 2.3 %copy-start.4 = (f32[1,4,8,16,128]{4,3,2,1,0:T(8,128)S(1)}, f32[1,4,8,16,128]{4,3,2,1,0:T(8,128)}, u32[]{:S(2)}) copy-start(f32[1,4,8,16,128]{4,3,2,1,0:T(8,128)} %copy.205) | copy-start | bytes 786436
  51.4 2.3 %copy-start.5 = (f32[1,4,8,16,128]{4,3,2,1,0:T(8,128)S(1)}, f32[1,4,8,16,128]{4,3,2,1,0:T(8,128)}, u32[]{:S(2)}) copy-start(f32[1,4,8,16,128]{4,3,2,1,0:T(8,128)} %copy.206) | copy-start | bytes 786436
  51.4 2.3 %copy-start.6 = (f32[1,4,8,16,128]{4,3,2,1,0:T(8,128)S(1)}, f32[1,4,8,16,128]{4,3,2,1,0:T(8,128)}, u32[]{:S(2)}) copy-start(f32[1,4,8,16,128]{4,3,2,1,0:T(8,128)} %copy.207) | copy-start | bytes 786436
  51.4 2.3 %copy-start.7 = (f32[1,4,8,16,128]{4,3,2,1,0:T(8,128)S(1)}, f32[1,4,8,16,128]{4,3,2,1,0:T(8,128)}, u32[]{:S(2)}) copy-start(f32[1,4,8,16,128]{4,3,2,1,0:T(8,128)} %copy.208) | copy-start | bytes 786436
  51.4 2.3 %copy-start.10 = (f32[1,4,128,128]{3,2,1,0:T(8,128)S(1)}, f32[1,4,128,128]{3,2,1,0:T(8,128)}, u32[]{:S(2)}) copy-start(f32[1,4,128,128]{3,2,1,0:T(8,128)} %param.9) | copy-start | bytes 786436
  51.4 2.3 %copy-start.11 = (f32[1,4,8,16,128]{4,3,2,1,0:T(8,128)S(1)}, f32[1,4,8,16,128]{4,3,2,1,0:T(8,128)}, u32[]{:S(2)}) copy-start(f32[1,4,8,16,128]{4,3,2,1,0:T(8,128)} %copy.209) | copy-start | bytes 786436
  54.4 1.8 %copy-start.8 = (f32[4,1,128,128]{3,2,0,1:T(8,128)}, f32[4,1,128,128]{3,2,0,1:T(8,128)S(1)}, u32[]{:S(2)}) copy-start(f32[4,1,128,128]{3,2,0,1:T(8,128)S(1)} %get-tuple-element.54) | copy-start | bytes 786436
  55.5 0.7 copy-start.13
  56.2 14.8 %all-to-all-start.2 = ((f32[8,1,4,16,128]{4,3,2,1,0:T(8,128)}), f32[8,1,4,16,128]{4,3,2,1,0:T(8,128)S(1)}, u32[]{:S(2)}, u32[]{:S(2)}) async-start(f32[8,1,4,16,128]{4,3,2,1,0:T(8,128)} %copy-done.13), calls=%async_computation.2 | async-start | bytes 524288 | tf_op jit(solution)/shard_map/all_to_all | solution.py:158
  62.3 9.3 %copy-start.12 = (f32[1,30,16,1]{3,2,1,0:T(8,128)S(1)}, f32[1,30,16,1]{3,2,1,0:T(8,128)}, u32[]{:S(2)}) copy-start(f32[1,30,16,1]{3,2,1,0:T(8,128)} %get-tuple-element.88) | copy-start | bytes 5764
  73.7 0.7 copy-start.14
